TPU v7x, 32 devices: a whole 2x2x4 slice. The times are simulated.
32 devices in a mesh: dp: 8 (over z, x), mp: 4 (over y, core).
Axes of the slice: x: 2, y: 2, z: 4, core: 2. Of those that a mesh axis runs over, the one named last changes fastest.
Arguments:
- tokens: bfloat16 [2, 16384, 768], P(None, ('dp', 'mp')), may hold values from -6 to 6
- segment_ids: int32 [2, 16384], P(None, 'dp'), may hold values from 0 to 63, never falling along the last dimension, each value on 1 to 768 neighbouring positions
- norm1_gain: float32 [768], replicated, may hold values from 0.1 to 1.9
- norm1_bias: float32 [768], replicated, may hold values from -3 to 3
- w_qkv: bfloat16 [768, 3, 768], replicated, may hold values from -0.21875 to 0.21875
- conv_weight: float32 [3, 3, 768], P(None, None, 'mp'), may hold values from -3 to 3
- w_out: bfloat16 [768, 768], replicated, may hold values from -1.75 to 1.75
- norm2_gain: float32 [768], replicated, may hold values from 0.1 to 1.9
- norm2_bias: float32 [768], replicated, may hold values from -3 to 3
- w_in: bfloat16 [768, 3072], replicated, may hold values from -0.21875 to 0.21875
- w_down: bfloat16 [3072, 768], replicated, may hold values from -0.109375 to 0.109375
- cotangent: bfloat16 [2, 16384, 768], P(None, ('dp', 'mp')), may hold values from -6 to 6
Outputs:
- output: bfloat16 [2, 16384, 768], P(None, ('dp', 'mp'))
- input_grad: float32 [2, 16384, 768], P(None, ('dp', 'mp'))
- norm1_gain_grad: float32 [768], P('mp')
- norm1_bias_grad: float32 [768], P('mp')
- qkv_grad: float32 [768, 3, 768], P(None, None, 'mp')
- conv_grad: float32 [3, 3, 768], P(None, None, 'mp')
- out_grad: float32 [768, 768], P('mp')
- norm2_gain_grad: float32 [768], P('mp')
- norm2_bias_grad: float32 [768], P('mp')
- in_grad: float32 [768, 3072], replicated
- down_grad: float32 [3072, 768], replicated
Inputs may be any that keep to these rules, and one draw needn't show every extreme that they name: `segment_ids`: segment numbers never fall along a row of 16384 tokens. A document may run on past the end of a sequence of 1024 tokens, but attention and the convolution still stop there, whatever the numbers.
All inputs are finite; a program needn't handle non-finite values.
Results may differ from a plain program's by a relative error of at most 0.015.
The roundings to bfloat16 on the way count: a program that leaves them out, or rounds other values in their place, can miss the bound.
Values may be sent and summed in bfloat16 or wider, within the bound.
No kernel may reach another device: no remote copies, remote signals or barrier semaphores. Data moves between devices by JAX's collectives and lax.ppermute only.
A program may use at most 256 MiB of HBM per device.

v0:
```python
import math
import jax
import jax.numpy as jnp
from jax import lax
from jax.sharding import PartitionSpec as P

HEAD_DIM = 64
LEN = 1024
EPSILON = 1e-05
MASKED = -1e30


def normalize(values, norm_gain, norm_bias):
    centred = values - jnp.mean(values, axis=-1, keepdims=True)
    rstd_row = lax.rsqrt(jnp.mean(centred * centred, axis=-1, keepdims=True) + EPSILON)
    scaled = centred * rstd_row
    return (scaled * norm_gain + norm_bias, scaled, rstd_row)


def normalize_back(gradient, scaled, rstd_row, norm_gain):
    grad_scaled = gradient * norm_gain
    inner_term = (
        grad_scaled
        - jnp.mean(grad_scaled, axis=-1, keepdims=True)
        - scaled * jnp.mean(grad_scaled * scaled, axis=-1, keepdims=True)
    )
    return (rstd_row * inner_term, jnp.sum(gradient * scaled, axis=0), jnp.sum(gradient, axis=0))


def delayed(values, shift_by):
    widths = [(shift_by, 0)] + [(0, 0)] * (values.ndim - 1)
    return jnp.pad(values, widths)[: values.shape[0]]


def advanced(values, shift_by):
    widths = [(0, shift_by)] + [(0, 0)] * (values.ndim - 1)
    return jnp.pad(values, widths)[shift_by:]


def score_block(queries_all, keys_all, seg_seqs, block_id, block_rows, scaling):
    per_seq = LEN // block_rows
    seq_id = block_id // per_seq
    first_row = block_id % per_seq * block_rows
    query_seq = lax.dynamic_index_in_dim(queries_all, seq_id, 0, keepdims=False)
    queries = lax.dynamic_slice_in_dim(query_seq, first_row, block_rows, 0)
    key_seq = lax.dynamic_index_in_dim(keys_all, seq_id, 0, keepdims=False)
    seg_seq = lax.dynamic_index_in_dim(seg_seqs, seq_id, 0, keepdims=False)
    seg_query = lax.dynamic_slice_in_dim(seg_seq, first_row, block_rows, 0)
    rows_at = first_row + lax.iota(jnp.int32, block_rows)
    cols_at = lax.iota(jnp.int32, LEN)
    allowed = (cols_at[None, :] <= rows_at[:, None]) & (seg_seq[None, :] == seg_query[:, None])
    scores = (
        jnp.einsum("qhd,khd->hqk", queries, key_seq, preferred_element_type=jnp.float32) * scaling
    )
    return (jnp.where(allowed[None], scores, MASKED), queries, key_seq, seq_id, first_row)


def attend_forward(queries_all, keys_all, values_all, seg_seqs, block_rows, scaling):
    block_count = queries_all.shape[0] * (LEN // block_rows)

    def forward_block(block_id):
        scores, queries, key_seq, seq_id, first_row = score_block(
            queries_all, keys_all, seg_seqs, block_id, block_rows, scaling
        )
        value_seq = lax.dynamic_index_in_dim(values_all, seq_id, 0, keepdims=False)
        row_top = jnp.max(scores, axis=-1, keepdims=True)
        weights = jnp.exp(scores - row_top)
        row_total = jnp.sum(weights, axis=-1, keepdims=True)
        probabilities = (weights / row_total).astype(jnp.bfloat16)
        attended = jnp.einsum(
            "hqk,khd->qhd", probabilities, value_seq, preferred_element_type=jnp.float32
        )
        return (
            attended.astype(jnp.bfloat16).reshape(block_rows, -1),
            (row_top + jnp.log(row_total))[..., 0],
        )

    return lax.map(forward_block, jnp.arange(block_count, dtype=jnp.int32))


def attend_backward(
    queries_all, keys_all, values_all, seg_seqs, row_lse, grad_heads, block_rows, scaling
):
    seq_count = queries_all.shape[0]
    per_seq = LEN // block_rows
    grad_seqs = grad_heads.reshape(queries_all.shape)

    def backward_block(block_id):
        scores, queries, key_seq, seq_id, first_row = score_block(
            queries_all, keys_all, seg_seqs, block_id, block_rows, scaling
        )
        value_seq = lax.dynamic_index_in_dim(values_all, seq_id, 0, keepdims=False)
        grad_seq = lax.dynamic_index_in_dim(grad_seqs, seq_id, 0, keepdims=False)
        grad_rows = lax.dynamic_slice_in_dim(grad_seq, first_row, block_rows, 0)
        lse_block = lax.dynamic_index_in_dim(row_lse, block_id, 0, keepdims=False)
        probabilities = jnp.exp(scores - lse_block[..., None])
        grad_probs = jnp.einsum(
            "qhd,khd->hqk", grad_rows, value_seq, preferred_element_type=jnp.float32
        )
        row_dot = jnp.sum(probabilities * grad_probs, axis=-1, keepdims=True)
        grad_scores = (probabilities * (grad_probs - row_dot)).astype(jnp.bfloat16)
        grad_queries = (
            jnp.einsum("hqk,khd->qhd", grad_scores, key_seq, preferred_element_type=jnp.float32)
            * scaling
        )
        grad_keys = (
            jnp.einsum("hqk,qhd->khd", grad_scores, queries, preferred_element_type=jnp.float32)
            * scaling
        )
        grad_values = jnp.einsum(
            "hqk,qhd->khd",
            probabilities.astype(jnp.bfloat16),
            grad_rows,
            preferred_element_type=jnp.float32,
        )
        return (grad_queries, grad_keys, grad_values)

    grad_queries, grad_keys, grad_values = lax.map(
        backward_block, jnp.arange(seq_count * per_seq, dtype=jnp.int32)
    )
    key_shape = (seq_count, per_seq) + grad_keys.shape[1:]
    grad_keys = jnp.sum(grad_keys.reshape(key_shape), axis=1)
    grad_values = jnp.sum(grad_values.reshape(key_shape), axis=1)
    return (grad_queries, grad_keys, grad_values)


def local(
    tokens,
    segment_ids,
    norm1_gain,
    norm1_bias,
    w_qkv,
    conv_weight,
    w_out,
    norm2_gain,
    norm2_bias,
    w_in,
    w_down,
    cotangent,
):
    micro_count = tokens.shape[0]
    group_rows = segment_ids.shape[1]
    local_width = conv_weight.shape[2]
    local_heads = local_width // HEAD_DIM
    seq_count = group_rows // LEN
    block_rows = min(512, LEN)
    scaling = 1.0 / math.sqrt(HEAD_DIM)
    places = lax.iota(jnp.int32, group_rows) % LEN
    kept = []
    outputs = []
    for micro_step in range(micro_count):
        token_rows = tokens[micro_step].astype(jnp.float32)
        normed_one, scaled_one, rstd_one = normalize(token_rows, norm1_gain, norm1_bias)
        normed_one = normed_one.astype(jnp.bfloat16)
        projected = jnp.einsum(
            "rd,dce->rce", normed_one, w_qkv, preferred_element_type=jnp.float32
        ).astype(jnp.bfloat16)
        by_heads = lax.all_to_all(projected, "mp", split_axis=2, concat_axis=0, tiled=True)
        seg_row = segment_ids[micro_step]
        same_one = ((places >= 1) & (delayed(seg_row, 1) == seg_row)).astype(jnp.float32)[
            :, None, None
        ]
        same_two = ((places >= 2) & (delayed(seg_row, 2) == seg_row)).astype(jnp.float32)[
            :, None, None
        ]
        heads_wide = by_heads.astype(jnp.float32)
        mixed = (
            heads_wide * conv_weight[:, 0]
            + delayed(heads_wide, 1) * same_one * conv_weight[:, 1]
            + delayed(heads_wide, 2) * same_two * conv_weight[:, 2]
        ).astype(jnp.bfloat16)
        shaped = mixed.reshape(seq_count, LEN, 3, local_heads, HEAD_DIM)
        queries_all = shaped[:, :, 0]
        keys_all = shaped[:, :, 1]
        values_all = shaped[:, :, 2]
        seg_seqs = seg_row.reshape(seq_count, LEN)
        attended, row_lse = attend_forward(
            queries_all, keys_all, values_all, seg_seqs, block_rows, scaling
        )
        attended = attended.reshape(group_rows, local_width)
        by_tokens = lax.all_to_all(attended, "mp", split_axis=0, concat_axis=1, tiled=True)
        resid = token_rows + jnp.dot(by_tokens, w_out, preferred_element_type=jnp.float32)
        normed_two, scaled_two, rstd_two = normalize(resid, norm2_gain, norm2_bias)
        normed_two = normed_two.astype(jnp.bfloat16)
        hidden_pre = jnp.dot(normed_two, w_in, preferred_element_type=jnp.float32)
        hidden = (jnp.maximum(hidden_pre, 0.0) ** 2).astype(jnp.bfloat16)
        outputs.append(
            (resid + jnp.dot(hidden, w_down, preferred_element_type=jnp.float32)).astype(
                jnp.bfloat16
            )
        )
        kept.append(
            (
                normed_one,
                scaled_one,
                rstd_one,
                heads_wide,
                same_one,
                same_two,
                queries_all,
                keys_all,
                values_all,
                seg_seqs,
                row_lse,
                by_tokens,
                normed_two,
                scaled_two,
                rstd_two,
                hidden_pre,
                hidden,
            )
        )
    grad_qkv = jnp.zeros(w_qkv.shape, jnp.float32)
    grad_conv = jnp.zeros(conv_weight.shape, jnp.float32)
    grad_wout = jnp.zeros(w_out.shape, jnp.float32)
    grad_in = jnp.zeros(w_in.shape, jnp.float32)
    grad_down = jnp.zeros(w_down.shape, jnp.float32)
    gain_one_grad = jnp.zeros(norm1_gain.shape, jnp.float32)
    bias_one_grad = jnp.zeros(norm1_bias.shape, jnp.float32)
    gain_two_grad = jnp.zeros(norm2_gain.shape, jnp.float32)
    bias_two_grad = jnp.zeros(norm2_bias.shape, jnp.float32)
    input_grads = [None] * micro_count
    for micro_step in reversed(range(micro_count)):
        (
            normed_one,
            scaled_one,
            rstd_one,
            heads_wide,
            same_one,
            same_two,
            queries_all,
            keys_all,
            values_all,
            seg_seqs,
            row_lse,
            by_tokens,
            normed_two,
            scaled_two,
            rstd_two,
            hidden_pre,
            hidden,
        ) = kept[micro_step]
        grad_output = cotangent[micro_step]
        grad_down = grad_down + jnp.einsum(
            "rf,rd->fd", hidden, grad_output, preferred_element_type=jnp.float32
        )
        grad_hidden = jnp.einsum(
            "rd,fd->rf", grad_output, w_down, preferred_element_type=jnp.float32
        )
        grad_pre = (grad_hidden * 2.0 * jnp.maximum(hidden_pre, 0.0)).astype(jnp.bfloat16)
        grad_in = grad_in + jnp.einsum(
            "rd,rf->df", normed_two, grad_pre, preferred_element_type=jnp.float32
        )
        grad_normed_two = jnp.einsum(
            "rf,df->rd", grad_pre, w_in, preferred_element_type=jnp.float32
        )
        back_two, gain_two_part, bias_two_part = normalize_back(
            grad_normed_two, scaled_two, rstd_two, norm2_gain
        )
        gain_two_grad = gain_two_grad + gain_two_part
        bias_two_grad = bias_two_grad + bias_two_part
        grad_resid = grad_output.astype(jnp.float32) + back_two
        grad_branch = grad_resid.astype(jnp.bfloat16)
        grad_wout = grad_wout + jnp.einsum(
            "re,rd->ed", by_tokens, grad_branch, preferred_element_type=jnp.float32
        )
        grad_attended = jnp.einsum(
            "rd,ed->re", grad_branch, w_out, preferred_element_type=jnp.float32
        ).astype(jnp.bfloat16)
        grad_heads = lax.all_to_all(grad_attended, "mp", split_axis=1, concat_axis=0, tiled=True)
        grad_queries, grad_keys, grad_values = attend_backward(
            queries_all, keys_all, values_all, seg_seqs, row_lse, grad_heads, block_rows, scaling
        )
        grad_mixed = jnp.stack(
            [
                grad_queries.reshape(group_rows, local_width),
                grad_keys.reshape(group_rows, local_width),
                grad_values.reshape(group_rows, local_width),
            ],
            axis=1,
        )
        weighted_one = grad_mixed * same_one
        weighted_two = grad_mixed * same_two
        grad_conv = grad_conv + jnp.stack(
            [
                jnp.sum(grad_mixed * heads_wide, axis=0),
                jnp.sum(weighted_one * delayed(heads_wide, 1), axis=0),
                jnp.sum(weighted_two * delayed(heads_wide, 2), axis=0),
            ],
            axis=1,
        )
        grad_proj = (
            grad_mixed * conv_weight[:, 0]
            + advanced(weighted_one, 1) * conv_weight[:, 1]
            + advanced(weighted_two, 2) * conv_weight[:, 2]
        ).astype(jnp.bfloat16)
        grad_tokens = lax.all_to_all(grad_proj, "mp", split_axis=0, concat_axis=2, tiled=True)
        grad_qkv = grad_qkv + jnp.einsum(
            "rd,rce->dce", normed_one, grad_tokens, preferred_element_type=jnp.float32
        )
        grad_normed_one = jnp.einsum(
            "rce,dce->rd", grad_tokens, w_qkv, preferred_element_type=jnp.float32
        )
        back_one, gain_one_part, bias_one_part = normalize_back(
            grad_normed_one, scaled_one, rstd_one, norm1_gain
        )
        gain_one_grad = gain_one_grad + gain_one_part
        bias_one_grad = bias_one_grad + bias_one_part
        input_grads[micro_step] = grad_resid + back_one
    head_parts = (
        lax.psum_scatter(
            grad_qkv.astype(jnp.bfloat16), "mp", scatter_dimension=2, tiled=True
        ).astype(jnp.float32),
        lax.psum_scatter(
            grad_wout.astype(jnp.bfloat16), "mp", scatter_dimension=0, tiled=True
        ).astype(jnp.float32),
        lax.psum_scatter(
            gain_one_grad.astype(jnp.bfloat16), "mp", scatter_dimension=0, tiled=True
        ).astype(jnp.float32),
        lax.psum_scatter(
            bias_one_grad.astype(jnp.bfloat16), "mp", scatter_dimension=0, tiled=True
        ).astype(jnp.float32),
        lax.psum_scatter(
            gain_two_grad.astype(jnp.bfloat16), "mp", scatter_dimension=0, tiled=True
        ).astype(jnp.float32),
        lax.psum_scatter(
            bias_two_grad.astype(jnp.bfloat16), "mp", scatter_dimension=0, tiled=True
        ).astype(jnp.float32),
    )
    head_total = lax.psum(
        (
            head_parts[0],
            head_parts[1],
            grad_conv,
            head_parts[2],
            head_parts[3],
            head_parts[4],
            head_parts[5],
        ),
        "dp",
    )
    dense_parts = (
        lax.psum_scatter(grad_in, ("dp", "mp"), scatter_dimension=1, tiled=True),
        lax.psum_scatter(grad_down, ("dp", "mp"), scatter_dimension=0, tiled=True),
    )
    dense_total = (
        lax.all_gather(
            dense_parts[0].astype(jnp.bfloat16), ("dp", "mp"), axis=1, tiled=True
        ).astype(jnp.float32),
        lax.all_gather(
            dense_parts[1].astype(jnp.bfloat16), ("dp", "mp"), axis=0, tiled=True
        ).astype(jnp.float32),
    )
    return (
        jnp.stack(outputs, axis=0),
        jnp.stack(input_grads, axis=0),
        head_total[3],
        head_total[4],
        head_total[0],
        head_total[2],
        head_total[1],
        head_total[5],
        head_total[6],
        dense_total[0],
        dense_total[1],
    )


def solution(mesh):
    placed = (
        P(None, ("dp", "mp"), None),
        P(None, "dp"),
        P(),
        P(),
        P(),
        P(None, None, "mp"),
        P(),
        P(),
        P(),
        P(),
        P(),
        P(None, ("dp", "mp"), None),
    )
    return jax.shard_map(
        local,
        mesh=mesh,
        in_specs=placed,
        out_specs=(
            P(None, ("dp", "mp"), None),
            P(None, ("dp", "mp"), None),
            P("mp"),
            P("mp"),
            P(None, None, "mp"),
            P(None, None, "mp"),
            P("mp", None),
            P("mp"),
            P("mp"),
            P(),
            P(),
        ),
        check_vma=False,
    )
```

profile of v0, /device:TPU:0, one launch (start us, length us, event | category | flops | bytes accessed | tf_op | source)
XLA Modules:
  0.0 973.8 jit_solution(13896892952462681706)
XLA Ops:
  15.4 6.0 copy.62
  31.3 6.0 copy.68
  37.3 26.4 %all-to-all-done = bf16[512,3,768]{0,1,2:T(4,128)(2,1)} async-done(((bf16[512,3,768]{0,1,2:T(4,128)(2,1)}), bf16[512,3,768]{0,1,2:T(4,128)(2,1)}, u32[]{:S(2)}, u32[]{:S(2)}) %all-to-all-start) | async-done | bytes 2359328 | tf_op jit(solution)/shard_map/all_to_all | solution.py:158
  82.7 22.8 %all-to-all-done.2 = bf16[512,3,768]{0,1,2:T(4,128)(2,1)} async-done(((bf16[512,3,768]{0,1,2:T(4,128)(2,1)}), bf16[512,3,768]{0,1,2:T(4,128)(2,1)}, u32[]{:S(2)}, u32[]{:S(2)}) %all-to-all-start.2) | async-done | bytes 2359328 | tf_op jit(solution)/shard_map/all_to_all | solution.py:158
  112.2 7.5 add_convert_fusion.2
  119.7 6.6 reshape.593
  134.7 49.8 %while.64 = (s32[]{:T(128)}, bf16[4,512,192]{1,2,0:T(8,128)(2,1)}, f32[4,3,512]{2,1,0:T(4,128)}, s32[4]{0:T(128)}, bf16[2,1024,3,64]{1,3,2,0:T(8,128)(2,1)}, /*i...) while((s32[]{:T(128)}, bf16[4,512,192]{1,2,0:T(8,128)(2,1)}, ...), condition=%wide.region_5.6_spmd, body=%wide.region_2.5_spmd.sunk | while | flops 423197728 | bytes 25768452 | solution.py:78
  188.7 6.6 reshape.594
  203.8 49.4 %while.65 = (s32[]{:T(128)}, bf16[4,512,192]{1,2,0:T(8,128)(2,1)}, f32[4,3,512]{2,1,0:T(4,128)}, s32[4]{0:T(128)}, bf16[2,1024,3,64]{1,3,2,0:T(8,128)(2,1)}, /*i...) while((s32[]{:T(128)}, bf16[4,512,192]{1,2,0:T(8,128)(2,1)}, ...), condition=%wide.region_13.14_spmd, body=%wide.region_10.13_spmd.sunk | while | flops 423197728 | bytes 25768452 | solution.py:78
  262.3 6.8 all-to-all-done.3
  280.1 8.6 multiply_convert_fusion.2
  294.0 5.8 fusion.233
  305.5 6.1 fusion.239
  311.7 6.7 multiply_reduce_fusion.6
  341.3 9.5 convolution_add_fusion
  369.1 79.1 %while.66 = (s32[]{:T(128)}, f32[4,512,3,64]{1,3,2,0:T(8,128)}, f32[4,1024,3,64]{1,3,2,0:T(8,128)}, f32[4,1024,3,64]{1,3,2,0:T(8,128)}, s32[4]{0:T(128)S(1)}, /*...) while((s32[]{:T(128)}, f32[4,512,3,64]{1,3,2,0:T(8,128)}, ...), condition=%wide.region_20.21_spmd, body=%wide.region_18.20_spmd.sunk | while | flops 1032092672 | bytes 62722712 | solution.py:118
  461.8 79.5 %while.67 = (s32[]{:T(128)}, f32[4,512,3,64]{1,3,2,0:T(8,128)}, f32[4,1024,3,64]{1,3,2,0:T(8,128)}, f32[4,1024,3,64]{1,3,2,0:T(8,128)}, s32[4]{0:T(128)S(1)}, /*...) while((s32[]{:T(128)}, f32[4,512,3,64]{1,3,2,0:T(8,128)}, ...), condition=%wide.region_29.30_spmd, body=%wide.region_27.29_spmd.sunk | while | flops 1032092672 | bytes 62722712 | solution.py:118
  592.5 5.9 multiply_reduce_fusion.5
  598.5 6.6 multiply_reduce_fusion.3
  605.1 10.6 %fusion.111 = (bf16[2048,3,192]{0,2,1:T(8,128)(2,1)}, bf16[2048,3,192]{0,2,1:T(8,128)(2,1)}) fusion(f32[2048,3,192]{0,2,1:T(8,128)} %get-tuple-element.888, f32[2048,3,192]{0,2,1:T(8,128)} %get-tuple-element.887, f32[2048,3,192]{0,2,1:T(8,128)S(1)} %constant_dynamic-update-slice_fusion.2, f32[3,192]{1,0:T(4,128)S(1)} %copy-done.63, ...), kind=kLoop, calls=%fused_computation.154 | loop fusion | flops 14155776 | bytes 33037056 | tf_op jit(solution)/shard_map/convert_element_type | solution.py:296
  615.7 7.0 copy.83
  627.5 6.9 copy.96
  634.5 41.3 %all-to-all-done.5 = bf16[2048,3,192]{2,1,0:T(4,128)(2,1)} async-done(((bf16[2048,3,192]{2,1,0:T(4,128)(2,1)}), bf16[2048,3,192]{2,1,0:T(4,128)(2,1)}, u32[]{:S(2)}, u32[]{:S(2)}) %all-to-all-start.5) | async-done | bytes 2359328 | tf_op jit(solution)/shard_map/all_to_all | solution.py:297
  686.3 6.9 copy.85
  693.3 41.9 %all-to-all-done.7 = bf16[2048,3,192]{2,1,0:T(4,128)(2,1)} async-done(((bf16[2048,3,192]{2,1,0:T(4,128)(2,1)}), bf16[2048,3,192]{2,1,0:T(4,128)(2,1)}, u32[]{:S(2)}, u32[]{:S(2)}) %all-to-all-start.7) | async-done | bytes 2359328 | tf_op jit(solution)/shard_map/all_to_all | solution.py:297
  735.2 7.0 copy.98
  755.9 8.9 fusion.167
  764.8 6.8 fusion.166
  806.9 6.5 all-reduce.17
  827.2 118.0 %all-reduce.19 = (f32[192]{0:T(256)}, f32[192]{0:T(256)}, f32[768,3,192]{0,2,1:T(8,128)}, f32[3,3,192]{2,0,1:T(4,128)}, f32[192,768]{1,0:T(8,128)}, /*index=5*/f32[192]{0:T(256)}, f32[192]{0:T(256)}) all-reduce(f32[192]{0:T(256)S(1)} %copy-done.91, f32[192]{0:T(256)} %dynamic-slice_convert_fusion.2, ...), channel_id=1, replica_groups=mesh['dp'=8,'mp'=4] {'dp'}, use_global_device_ids=true, to_apply=%region_37.38 | all-reduce | flops 592320 | bytes 3558912 | tf_op jit(solution)/shard_map/psum | solution.py:330
  946.5 7.5 copy.109
  959.7 6.8 convert_element_type.321
  (601 shorter events, 489.1 us)
Async XLA Ops:
  9.0 17.0 %copy-start.70 = (f32[512]{0:T(512)}, f32[512]{0:T(512)S(1)}, u32[]{:S(2)}) copy-start(f32[512]{0:T(512)S(1)} %get-tuple-element.932) | copy-start | bytes 6148
  21.4 42.3 %all-to-all-start = ((bf16[512,3,768]{0,1,2:T(4,128)(2,1)}), bf16[512,3,768]{0,1,2:T(4,128)(2,1)}, u32[]{:S(2)}, u32[]{:S(2)}) async-start(bf16[512,3,768]{0,1,2:T(4,128)(2,1)} %copy.62), calls=%async_computation | async-start | bytes 6291456 | tf_op jit(solution)/shard_map/all_to_all | solution.py:158
  37.3 31.3 %copy-start.87 = (f32[3,3,192]{2,1,0:T(4,128)S(1)}, f32[3,3,192]{2,1,0:T(4,128)}, u32[]{:S(2)}) copy-start(f32[3,3,192]{2,1,0:T(4,128)} %param.25) | copy-start | bytes 20740
  63.7 41.8 %all-to-all-start.2 = ((bf16[512,3,768]{0,1,2:T(4,128)(2,1)}), bf16[512,3,768]{0,1,2:T(4,128)(2,1)}, u32[]{:S(2)}, u32[]{:S(2)}) async-start(bf16[512,3,768]{0,1,2:T(4,128)(2,1)} %copy.68), calls=%async_computation.2 | async-start | bytes 6291456 | tf_op jit(solution)/shard_map/all_to_all | solution.py:158
  110.7 9.0 copy-start.3
  184.5 68.8 %all-to-all-start.1 = ((bf16[4,512,192]{1,2,0:T(8,128)(2,1)}), bf16[4,512,192]{1,2,0:T(8,128)(2,1)}, u32[]{:S(2)}, u32[]{:S(2)}) async-start(bf16[4,512,192]{1,2,0:T(8,128)(2,1)} %get-tuple-element.653), calls=%async_computation.1 | async-start | bytes 1572864 | tf_op jit(solution)/shard_map/all_to_all | solution.py:181
  253.2 7.1 copy-start.45
  253.3 15.9 %all-to-all-start.3 = ((bf16[4,512,192]{1,2,0:T(8,128)(2,1)}), bf16[4,512,192]{1,2,0:T(8,128)(2,1)}, u32[]{:S(2)}, u32[]{:S(2)}) async-start(bf16[4,512,192]{1,2,0:T(8,128)(2,1)} %get-tuple-element.654), calls=%async_computation.3 | async-start | bytes 1572864 | tf_op jit(solution)/shard_map/all_to_all | solution.py:181
  257.5 493.8 %reduce-scatter.9.cloned.1.call-start = ((), (), s32[]{:S(2)}) async-start(), calls=%async_computation.14 | async-start | bytes 9732096 | tf_op jit(solution)/shard_map/reduce_scatter | solution.py:343
  269.2 8.1 slice-start.6
  271.9 22.0 %copy-start.29 = (f32[512,768]{1,0:T(8,128)}, f32[512,768]{1,0:T(8,128)S(1)}, u32[]{:S(2)}) copy-start(f32[512,768]{1,0:T(8,128)S(1)} %get-tuple-element.927) | copy-start | bytes 4718596
  271.9 22.0 %copy-start.68 = (f32[512]{0:T(512)}, f32[512]{0:T(512)S(1)}, u32[]{:S(2)}) copy-start(f32[512]{0:T(512)S(1)} %broadcast_multiply_fusion.12) | copy-start | bytes 6148
  272.3 21.7 %copy-start.85 = (f32[512]{0:T(512)}, f32[512]{0:T(512)S(1)}, u32[]{:S(2)}) copy-start(f32[512]{0:T(512)S(1)} %add_rsqrt_fusion) | copy-start | bytes 6148
  280.1 8.6 copy-start.8
  311.7 6.7 copy-start.27
  325.8 25.0 %all-to-all-start.4 = ((bf16[512,4,192]{0,2,1:T(8,128)(2,1)}), bf16[512,4,192]{0,2,1:T(8,128)(2,1)}, u32[]{:S(2)}, u32[]{:S(2)}) async-start(bf16[512,4,192]{0,2,1:T(8,128)(2,1)} %bitcast.519), calls=%async_computation.4 | async-start | bytes 1572864 | tf_op jit(solution)/shard_map/all_to_all | solution.py:270
  330.0 423.0 %reduce-scatter.11.cloned.1.call-start = ((), (), s32[]{:S(2)}) async-start(), calls=%async_computation.16 | async-start | bytes 9732096 | tf_op jit(solution)/shard_map/reduce_scatter | solution.py:344
  350.8 97.4 %all-to-all-start.6 = ((bf16[512,4,192]{0,2,1:T(8,128)(2,1)}), bf16[512,4,192]{0,2,1:T(8,128)(2,1)}, u32[]{:S(2)}, u32[]{:S(2)}) async-start(bf16[512,4,192]{0,2,1:T(8,128)(2,1)} %bitcast.518), calls=%async_computation.6 | async-start | bytes 1572864 | tf_op jit(solution)/shard_map/all_to_all | solution.py:270
  591.7 6.7 slice-start.2
  598.4 6.6 copy-start.61
  598.4 6.6 copy-start.63
  622.7 53.1 %all-to-all-start.5 = ((bf16[2048,3,192]{2,1,0:T(4,128)(2,1)}), bf16[2048,3,192]{2,1,0:T(4,128)(2,1)}, u32[]{:S(2)}, u32[]{:S(2)}) async-start(bf16[2048,3,192]{2,1,0:T(4,128)(2,1)} %copy.83), calls=%async_computation.5 | async-start | bytes 8388608 | tf_op jit(solution)/shard_map/all_to_all | solution.py:297
  675.7 59.4 %all-to-all-start.7 = ((bf16[2048,3,192]{2,1,0:T(4,128)(2,1)}), bf16[2048,3,192]{2,1,0:T(4,128)(2,1)}, u32[]{:S(2)}, u32[]{:S(2)}) async-start(bf16[2048,3,192]{2,1,0:T(4,128)(2,1)} %copy.96), calls=%async_computation.7 | async-start | bytes 8388608 | tf_op jit(solution)/shard_map/all_to_all | solution.py:297
  680.6 115.9 %reduce-scatter.7.cloned.1.call-start = ((), (), s32[]{:S(2)}) async-start(), calls=%async_computation.13 | async-start | bytes 1474560 | tf_op jit(solution)/shard_map/reduce_scatter | solution.py:314
  686.3 140.9 %reduce-scatter.5.cloned.1.call-start = ((), (), s32[]{:S(2)}) async-start(), calls=%async_computation.12 | async-start | bytes 4423680 | tf_op jit(solution)/shard_map/reduce_scatter | solution.py:311
  735.2 7.0 copy-start.71
  735.2 7.1 copy-start.83
  735.2 7.1 copy-start.89
  735.2 7.1 copy-start.98
  751.2 195.3 %all-gather.3.cloned.1.call-start = ((), (), s32[]{:S(2)}) async-start(), calls=%async_computation.15 | async-start | bytes 4866048 | tf_op jit(solution)/shard_map/all_gather | solution.py:347
  752.9 206.8 %all-gather.5.cloned.1.call-start = ((), (), s32[]{:S(2)}) async-start(), calls=%async_computation.17 | async-start | bytes 4866048 | tf_op jit(solution)/shard_map/all_gather | solution.py:350
  755.9 8.9 copy-start.19
  (114 other events, 336.0 us)
Sparse Core Ops, SparseCore 0:
  305.6 141.4 reduce-scatter.8
  453.6 135.1 reduce-scatter.10
  686.4 34.4 reduce-scatter.6
  751.3 41.3 reduce-scatter.4
  795.5 82.9 all-gather.2
  881.2 78.4 all-gather.4
where the time goes:
time: 984 us; the launch traced here: 974 us
  matrix products  254 us (26%)
  local copies, waits for them, and re-layouts  225 us (23%)
  waiting for transfers between devices  145 us (15%)
  blocking collectives  125 us (13%)
  other arithmetic  118 us (12%)
  loops' own time  53.9 us (5%)
  starting transfers between devices  36.9 us (4%)
  between operations  16.6 us (2%)
    psum x1, blocking collectives, local(): lax.psum((head_parts[0], head_parts[1], grad_conv, head_parts[2], head_pa...  118 us
    all_to_all x2, waiting for transfers between devices, local(): lax.all_to_all(grad_proj, 'mp', split_axis=0, concat_axis=2, tiled=True)  83.2 us
    all_to_all x2, waiting for transfers between devices, local(): lax.all_to_all(projected, 'mp', split_axis=2, concat_axis=0, tiled=True)  49.3 us
    dot_general x16, matrix products, score_block(): jnp.einsum('qhd,khd->hqk', queries, key_seq, preferred_element_type=jnp.f...  39.8 us
    another operation x16, local copies, waits for them, and re-layouts, local(): jnp.stack([grad_queries.reshape(group_rows, local_width), grad_keys.resha...  39 us
    another operation x2, loops' own time, attend_backward(): lax.map(backward_block, jnp.arange(seq_count * per_seq, dtype=jnp.int32))  32.2 us
    unnamed x209, local copies, waits for them, and re-layouts  27.9 us
    dot_general x8, matrix products, backward_block(): jnp.einsum('hqk,qhd->khd', probabilities.astype(jnp.bfloat16), grad_rows,...  22.4 us
  transfers between devices with their start and end apart: 14, of which 6 were waited for; matrix products, arithmetic and copies ran while one was open for 48% of the time, Pallas kernels for 0%

commit v1 on v0

--- a/solution.py
+++ b/solution.py
@@ -294,7 +294,12 @@
             + advanced(weighted_one, 1) * conv_weight[:, 1]
             + advanced(weighted_two, 2) * conv_weight[:, 2]
         ).astype(jnp.bfloat16)
-        grad_tokens = lax.all_to_all(grad_proj, "mp", split_axis=0, concat_axis=2, tiled=True)
+        grad_tokens = jnp.concatenate(
+            lax.all_to_all(
+                jnp.stack(jnp.split(grad_proj, lax.axis_size("mp"), axis=0)), "mp", 0, 0
+            ),
+            axis=2,
+        )
         grad_qkv = grad_qkv + jnp.einsum(
             "rd,rce->dce", normed_one, grad_tokens, preferred_element_type=jnp.float32
         )

time: 984 us -> 927 us (0.942)
  waiting for transfers between devices: 145 us -> 109 us
  local copies, waits for them, and re-layouts: 225 us -> 204 us
    all_to_all x2, waiting for transfers between devices: 83.2 us -> 47.2 us  [local(): lax.all_to_all(jnp.stack(jnp.split(grad_proj, lax.axis_size('mp'), axis=0...]
    all_to_all x2 -> x0, local copies, waits for them, and re-layouts: 14 us -> none  [local(): lax.all_to_all(grad_proj, 'mp', split_axis=0, concat_axis=2, tiled=True)]
    convert_element_type x2 -> x0, local copies, waits for them, and re-layouts: 13.9 us -> none  [local(): grad_proj = (grad_mixed * conv_weight[:, 0] + advanced(weighted_one, 1) *...]
    unnamed x209 -> x211, local copies, waits for them, and re-layouts: 27.9 us -> 28.1 us
where the time goes in v1:
time: 927 us; the launch traced here: 917 us
  matrix products  251 us (27%)
  local copies, waits for them, and re-layouts  204 us (22%)
  blocking collectives  126 us (14%)
  other arithmetic  122 us (13%)
  waiting for transfers between devices  109 us (12%)
  loops' own time  53.9 us (6%)
  starting transfers between devices  36.2 us (4%)
  between operations  16.7 us (2%)
    psum x1, blocking collectives, local(): lax.psum((head_parts[0], head_parts[1], grad_conv, head_parts[2], head_pa...  119 us
    all_to_all x2, waiting for transfers between devices, local(): lax.all_to_all(projected, 'mp', split_axis=2, concat_axis=0, tiled=True)  49.2 us
    all_to_all x2, waiting for transfers between devices, local(): lax.all_to_all(jnp.stack(jnp.split(grad_proj, lax.axis_size('mp'), axis=0...  47.2 us
    dot_general x16, matrix products, score_block(): jnp.einsum('qhd,khd->hqk', queries, key_seq, preferred_element_type=jnp.f...  39.7 us
    another operation x16, local copies, waits for them, and re-layouts, local(): jnp.stack([grad_queries.reshape(group_rows, local_width), grad_keys.resha...  39 us
    another operation x2, loops' own time, attend_backward(): lax.map(backward_block, jnp.arange(seq_count * per_seq, dtype=jnp.int32))  32.2 us
    unnamed x211, local copies, waits for them, and re-layouts  28.1 us
    dot_general x8, matrix products, backward_block(): jnp.einsum('hqk,qhd->khd', probabilities.astype(jnp.bfloat16), grad_rows,...  22.4 us
  transfers between devices with their start and end apart: 14, of which 6 were waited for; matrix products, arithmetic and copies ran while one was open for 48% of the time, Pallas kernels for 0%

profile of v1, /device:TPU:0, one launch (start us, length us, event | category | flops | bytes accessed | tf_op | source)
XLA Modules:
  0.0 917.3 jit_solution(8295530578231400474)
XLA Ops:
  15.4 6.0 copy.66
  31.3 6.0 copy.72
  37.3 26.4 %all-to-all-done = bf16[512,3,768]{0,1,2:T(4,128)(2,1)} async-done(((bf16[512,3,768]{0,1,2:T(4,128)(2,1)}), bf16[512,3,768]{0,1,2:T(4,128)(2,1)}, u32[]{:S(2)}, u32[]{:S(2)}) %all-to-all-start) | async-done | bytes 2359328 | tf_op jit(solution)/shard_map/all_to_all | solution.py:158
  82.7 22.8 %all-to-all-done.2 = bf16[512,3,768]{0,1,2:T(4,128)(2,1)} async-done(((bf16[512,3,768]{0,1,2:T(4,128)(2,1)}), bf16[512,3,768]{0,1,2:T(4,128)(2,1)}, u32[]{:S(2)}, u32[]{:S(2)}) %all-to-all-start.2) | async-done | bytes 2359328 | tf_op jit(solution)/shard_map/all_to_all | solution.py:158
  112.2 7.5 add_convert_fusion.2
  119.7 6.6 reshape.605
  134.7 49.8 %while.64 = (s32[]{:T(128)}, bf16[4,512,192]{1,2,0:T(8,128)(2,1)}, f32[4,3,512]{2,1,0:T(4,128)}, s32[4]{0:T(128)}, bf16[2,1024,3,64]{1,3,2,0:T(8,128)(2,1)}, /*i...) while((s32[]{:T(128)}, bf16[4,512,192]{1,2,0:T(8,128)(2,1)}, ...), condition=%wide.region_5.6_spmd, body=%wide.region_2.5_spmd.sunk | while | flops 423197728 | bytes 25768452 | solution.py:78
  188.7 6.6 reshape.606
  203.8 49.4 %while.65 = (s32[]{:T(128)}, bf16[4,512,192]{1,2,0:T(8,128)(2,1)}, f32[4,3,512]{2,1,0:T(4,128)}, s32[4]{0:T(128)}, bf16[2,1024,3,64]{1,3,2,0:T(8,128)(2,1)}, /*i...) while((s32[]{:T(128)}, bf16[4,512,192]{1,2,0:T(8,128)(2,1)}, ...), condition=%wide.region_13.14_spmd, body=%wide.region_10.13_spmd.sunk | while | flops 423197728 | bytes 25768452 | solution.py:78
  262.3 6.8 all-to-all-done.3
  280.1 8.6 multiply_convert_fusion.2
  288.7 5.2 multiply_convert_fusion.3
  294.0 5.8 fusion.233
  299.8 5.6 convolution_add_fusion.1
  305.5 6.1 fusion.239
  311.7 6.7 multiply_reduce_fusion.6
  335.9 5.3 fusion.168
  341.2 9.5 %convolution_add_fusion = f32[3072,768]{1,0:T(8,128)} fusion(f32[3072,768]{1,0:T(8,128)S(1)} %fusion.168, f32[512,3072]{1,0:T(8,128)} %copy-done.8, bf16[2,512,768]{2,1,0:T(8,128)(2,1)S(1)} %copy-done.28), kind=kOutput, calls=%fused_computation.141 | convolution fusion | flops 2422996992 | bytes 25952256 | tf_op jit(solution)/shard_map/rf,rd->fd/dot_general | solution.py:244
  369.0 79.1 %while.66 = (s32[]{:T(128)}, f32[4,512,3,64]{1,3,2,0:T(8,128)}, f32[4,1024,3,64]{1,3,2,0:T(8,128)}, f32[4,1024,3,64]{1,3,2,0:T(8,128)}, s32[4]{0:T(128)S(1)}, /*...) while((s32[]{:T(128)}, f32[4,512,3,64]{1,3,2,0:T(8,128)}, ...), condition=%wide.region_20.21_spmd, body=%wide.region_18.20_spmd.sunk | while | flops 1032092672 | bytes 62722712 | solution.py:118
  461.7 79.5 %while.67 = (s32[]{:T(128)}, f32[4,512,3,64]{1,3,2,0:T(8,128)}, f32[4,1024,3,64]{1,3,2,0:T(8,128)}, f32[4,1024,3,64]{1,3,2,0:T(8,128)}, s32[4]{0:T(128)S(1)}, /*...) while((s32[]{:T(128)}, f32[4,512,3,64]{1,3,2,0:T(8,128)}, ...), condition=%wide.region_29.30_spmd, body=%wide.region_27.29_spmd.sunk | while | flops 1032092672 | bytes 62722712 | solution.py:118
  592.3 6.0 multiply_reduce_fusion.5
  598.4 6.7 multiply_reduce_fusion.3
  605.1 10.2 %fusion.111 = (bf16[2048,3,192]{0,2,1:T(8,128)(2,1)S(1)}, bf16[2048,3,192]{0,2,1:T(8,128)(2,1)}) fusion(f32[2048,3,192]{0,2,1:T(8,128)} %get-tuple-element.888, f32[2048,3,192]{0,2,1:T(8,128)} %get-tuple-element.887, f32[2048,3,192]{0,2,1:T(8,128)S(1)} %constant_dynamic-update-slice_fusion.2, f32[3,192]{1,0:T(4,128)S(1)} %copy-done.64, ...), kind=kLoop, calls=%fused_computation.154 | loop fusion | flops 14155776 | bytes 33037056 | tf_op jit(solution)/shard_map/convert_element_type | solution.py:296
  625.2 25.1 %all-to-all-done.5 = bf16[4,512,3,192]{1,3,2,0:T(8,128)(2,1)} async-done(((bf16[4,512,3,192]{1,3,2,0:T(8,128)(2,1)}), bf16[4,512,3,192]{1,3,2,0:T(8,128)(2,1)}, u32[]{:S(2)}, u32[]{:S(2)}) %all-to-all-start.5) | async-done | bytes 2359328 | tf_op jit(solution)/shard_map/all_to_all | solution.py:298
  663.7 22.2 %all-to-all-done.7 = bf16[4,512,3,192]{1,3,2,0:T(8,128)(2,1)} async-done(((bf16[4,512,3,192]{1,3,2,0:T(8,128)(2,1)}), bf16[4,512,3,192]{1,3,2,0:T(8,128)(2,1)}, u32[]{:S(2)}, u32[]{:S(2)}) %all-to-all-start.7) | async-done | bytes 2359328 | tf_op jit(solution)/shard_map/all_to_all | solution.py:298
  699.6 8.1 fusion.167
  707.8 6.8 fusion.166
  743.4 5.1 fusion.154
  749.7 6.9 all-reduce.17
  770.4 118.9 %all-reduce.19 = (f32[192]{0:T(256)}, f32[192]{0:T(256)}, f32[768,3,192]{0,2,1:T(8,128)}, f32[3,3,192]{2,0,1:T(4,128)}, f32[192,768]{1,0:T(8,128)}, /*index=5*/f32[192]{0:T(256)}, f32[192]{0:T(256)}) all-reduce(f32[192]{0:T(256)S(1)} %copy-done.92, f32[192]{0:T(256)} %dynamic-slice_convert_fusion.2, ...), channel_id=1, replica_groups=mesh['dp'=8,'mp'=4] {'dp'}, use_global_device_ids=true, to_apply=%region_37.38 | all-reduce | flops 592320 | bytes 3558912 | tf_op jit(solution)/shard_map/psum | solution.py:335
  890.6 7.5 copy.109
  903.2 6.8 convert_element_type.321
  (605 shorter events, 475.1 us)
Async XLA Ops:
  9.0 17.0 %copy-start.71 = (f32[512]{0:T(512)}, f32[512]{0:T(512)S(1)}, u32[]{:S(2)}) copy-start(f32[512]{0:T(512)S(1)} %get-tuple-element.940) | copy-start | bytes 6148
  21.4 42.3 %all-to-all-start = ((bf16[512,3,768]{0,1,2:T(4,128)(2,1)}), bf16[512,3,768]{0,1,2:T(4,128)(2,1)}, u32[]{:S(2)}, u32[]{:S(2)}) async-start(bf16[512,3,768]{0,1,2:T(4,128)(2,1)} %copy.66), calls=%async_computation | async-start | bytes 6291456 | tf_op jit(solution)/shard_map/all_to_all | solution.py:158
  37.3 31.2 %copy-start.88 = (f32[3,3,192]{2,1,0:T(4,128)S(1)}, f32[3,3,192]{2,1,0:T(4,128)}, u32[]{:S(2)}) copy-start(f32[3,3,192]{2,1,0:T(4,128)} %param.25) | copy-start | bytes 20740
  63.7 41.8 %all-to-all-start.2 = ((bf16[512,3,768]{0,1,2:T(4,128)(2,1)}), bf16[512,3,768]{0,1,2:T(4,128)(2,1)}, u32[]{:S(2)}, u32[]{:S(2)}) async-start(bf16[512,3,768]{0,1,2:T(4,128)(2,1)} %copy.72), calls=%async_computation.2 | async-start | bytes 6291456 | tf_op jit(solution)/shard_map/all_to_all | solution.py:158
  110.7 9.0 copy-start.3
  184.5 68.7 %all-to-all-start.1 = ((bf16[4,512,192]{1,2,0:T(8,128)(2,1)}), bf16[4,512,192]{1,2,0:T(8,128)(2,1)}, u32[]{:S(2)}, u32[]{:S(2)}) async-start(bf16[4,512,192]{1,2,0:T(8,128)(2,1)} %get-tuple-element.653), calls=%async_computation.1 | async-start | bytes 1572864 | tf_op jit(solution)/shard_map/all_to_all | solution.py:181
  253.2 7.1 copy-start.46
  253.2 15.9 %all-to-all-start.3 = ((bf16[4,512,192]{1,2,0:T(8,128)(2,1)}), bf16[4,512,192]{1,2,0:T(8,128)(2,1)}, u32[]{:S(2)}, u32[]{:S(2)}) async-start(bf16[4,512,192]{1,2,0:T(8,128)(2,1)} %get-tuple-element.654), calls=%async_computation.3 | async-start | bytes 1572864 | tf_op jit(solution)/shard_map/all_to_all | solution.py:181
  257.4 437.5 %reduce-scatter.9.cloned.1.call-start = ((), (), s32[]{:S(2)}) async-start(), calls=%async_computation.14 | async-start | bytes 9732096 | tf_op jit(solution)/shard_map/reduce_scatter | solution.py:348
  269.1 8.1 slice-start.6
  271.9 22.0 %copy-start.29 = (f32[512,768]{1,0:T(8,128)}, f32[512,768]{1,0:T(8,128)S(1)}, u32[]{:S(2)}) copy-start(f32[512,768]{1,0:T(8,128)S(1)} %get-tuple-element.935) | copy-start | bytes 4718596
  271.9 22.0 %copy-start.69 = (f32[512]{0:T(512)}, f32[512]{0:T(512)S(1)}, u32[]{:S(2)}) copy-start(f32[512]{0:T(512)S(1)} %broadcast_multiply_fusion.12) | copy-start | bytes 6148
  272.3 21.7 %copy-start.86 = (f32[512]{0:T(512)}, f32[512]{0:T(512)S(1)}, u32[]{:S(2)}) copy-start(f32[512]{0:T(512)S(1)} %add_rsqrt_fusion) | copy-start | bytes 6148
  280.1 8.6 copy-start.8
  325.6 25.0 %all-to-all-start.4 = ((bf16[512,4,192]{0,2,1:T(8,128)(2,1)}), bf16[512,4,192]{0,2,1:T(8,128)(2,1)}, u32[]{:S(2)}, u32[]{:S(2)}) async-start(bf16[512,4,192]{0,2,1:T(8,128)(2,1)} %bitcast.529), calls=%async_computation.4 | async-start | bytes 1572864 | tf_op jit(solution)/shard_map/all_to_all | solution.py:270
  329.9 366.8 %reduce-scatter.11.cloned.1.call-start = ((), (), s32[]{:S(2)}) async-start(), calls=%async_computation.16 | async-start | bytes 9732096 | tf_op jit(solution)/shard_map/reduce_scatter | solution.py:349
  350.7 97.3 %all-to-all-start.6 = ((bf16[512,4,192]{0,2,1:T(8,128)(2,1)}), bf16[512,4,192]{0,2,1:T(8,128)(2,1)}, u32[]{:S(2)}, u32[]{:S(2)}) async-start(bf16[512,4,192]{0,2,1:T(8,128)(2,1)} %bitcast.528), calls=%async_computation.6 | async-start | bytes 1572864 | tf_op jit(solution)/shard_map/all_to_all | solution.py:270
  591.6 6.8 slice-start.2
  598.4 6.8 copy-start.62
  598.4 6.8 copy-start.64
  598.4 6.7 copy-start.66
  617.2 33.1 %all-to-all-start.5 = ((bf16[4,512,3,192]{1,3,2,0:T(8,128)(2,1)}), bf16[4,512,3,192]{1,3,2,0:T(8,128)(2,1)}, u32[]{:S(2)}, u32[]{:S(2)}) async-start(bf16[4,512,3,192]{1,3,2,0:T(8,128)(2,1)} %pad_maximum_fusion.1), calls=%async_computation.5 | async-start | bytes 4718592 | tf_op jit(solution)/shard_map/all_to_all | solution.py:298
  650.3 35.6 %all-to-all-start.7 = ((bf16[4,512,3,192]{1,3,2,0:T(8,128)(2,1)}), bf16[4,512,3,192]{1,3,2,0:T(8,128)(2,1)}, u32[]{:S(2)}, u32[]{:S(2)}) async-start(bf16[4,512,3,192]{1,3,2,0:T(8,128)(2,1)} %pad_maximum_fusion.2), calls=%async_computation.7 | async-start | bytes 4718592 | tf_op jit(solution)/shard_map/all_to_all | solution.py:298
  654.8 84.6 %reduce-scatter.7.cloned.1.call-start = ((), (), s32[]{:S(2)}) async-start(), calls=%async_computation.13 | async-start | bytes 1474560 | tf_op jit(solution)/shard_map/reduce_scatter | solution.py:319
  660.4 110.0 %reduce-scatter.5.cloned.1.call-start = ((), (), s32[]{:S(2)}) async-start(), calls=%async_computation.12 | async-start | bytes 4423680 | tf_op jit(solution)/shard_map/reduce_scatter | solution.py:316
  663.7 24.2 %copy-start.72 = (f32[512]{0:T(512)S(1)}, f32[512]{0:T(512)}, u32[]{:S(2)}) copy-start(f32[512]{0:T(512)} %copy-done.71) | copy-start | bytes 6148
  663.7 24.3 %copy-start.84 = (f32[512]{0:T(512)S(1)}, f32[512]{0:T(512)}, u32[]{:S(2)}) copy-start(f32[512]{0:T(512)} %copy-done.83) | copy-start | bytes 6148
  663.7 24.3 %copy-start.90 = (f32[768]{0:T(1024)S(1)}, f32[768]{0:T(1024)}, u32[]{:S(2)}) copy-start(f32[768]{0:T(1024)} %param.22) | copy-start | bytes 9220
  663.7 24.3 %copy-start.99 = (f32[768]{0:T(1024)S(1)}, f32[768]{0:T(1024)}, u32[]{:S(2)}) copy-start(f32[768]{0:T(1024)} %param.23) | copy-start | bytes 9220
  694.9 195.7 %all-gather.3.cloned.1.call-start = ((), (), s32[]{:S(2)}) async-start(), calls=%async_computation.15 | async-start | bytes 4866048 | tf_op jit(solution)/shard_map/all_gather | solution.py:352
  696.6 206.6 %all-gather.5.cloned.1.call-start = ((), (), s32[]{:S(2)}) async-start(), calls=%async_computation.17 | async-start | bytes 4866048 | tf_op jit(solution)/shard_map/all_gather | solution.py:355
  699.6 8.1 copy-start.19
  (115 other events, 330.1 us)
Sparse Core Ops, SparseCore 0:
  305.6 141.3 reduce-scatter.8
  453.5 135.0 reduce-scatter.10
  660.6 30.0 reduce-scatter.6
  695.0 42.4 reduce-scatter.4
  740.3 82.9 all-gather.2
  826.0 77.1 all-gather.4
